TPU v7x, 256 devices: a whole 4x4x8 slice. The times are simulated.
256 devices in a mesh: doc: 64 (over z, y, core), tp: 4 (over x).
Axes of the slice: x: 4, y: 4, z: 8, core: 2. Of those that a mesh axis runs over, the one named last changes fastest.
Arguments:
- storage: bfloat16 [32768, 3584], P('doc', 'tp'), may hold values from -40 to 40
- row_doc: int32 [32768], P('doc'), may hold values from -1 to 63, as said below
- row_pos: int32 [32768], P('doc'), may hold values from -1 to 511, as said below
- doc_len: int32 [64], replicated, may hold values from 64 to 512, as said below
- partner: int32 [64], replicated, may hold values from 0 to 63, as said below
- norm_gain: bfloat16 [3584], replicated, may hold values from 0.25 to 1.75
- qkv_weight: bfloat16 [3584, 4608], P('doc', 'tp'), may hold values from -0.09375 to 0.09375
- qkv_bias: bfloat16 [4608], P('tp'), may hold values from -24 to 24
Outputs:
- attention: bfloat16 [65536, 3584], P('doc', 'tp')
Inputs may be any that keep to these rules, and one draw needn't show every extreme that they name: `row_doc`: the rows 0 to doc_len[d] - 1 of each document d are stored exactly once over all devices, one to a slot; -1 marks an empty slot. One device stores at most 8 rows of any one document, and exactly 8 rows of a document of 512 tokens. `row_pos`: -1 for an empty slot. `doc_len`: some document has 512 tokens and some has 64. partner[partner[d]] = d and partner[d] != d.
All inputs are finite; a program needn't handle non-finite values.
Results may differ from a plain program's by a relative error of at most 0.008.
The roundings to bfloat16 on the way count: a program that leaves them out, or rounds other values in their place, can miss the bound.
Values may be sent and summed in bfloat16 or wider, within the bound.
A program may use at most 64 MiB of HBM per device.

v0:
```python
import jax
import jax.numpy as jnp
from jax import lax
from jax.sharding import PartitionSpec as P

HEADS = 28
KVH = 4
HD = 128
HALF = 512


ROPE_BASE = 1000000.0
EPSILON = 1e-06
BLOCK_ROWS = 512


def from_partner(value, axis, stride):
    mask = 2**stride
    pairs = [(source, source ^ mask) for source in range(lax.axis_size(axis))]
    return lax.ppermute(value, axis, pairs)


def pairing(partner):
    doc_ids = jnp.arange(partner.shape[0], dtype=jnp.int32)
    first_flag = (doc_ids < partner).astype(jnp.int32)
    before = jnp.cumsum(first_flag) - first_flag
    low_doc = jnp.minimum(doc_ids, partner)
    pick_mask = (low_doc[:, None] == doc_ids[None, :]).astype(jnp.int32)
    pair_index = jnp.sum(pick_mask * before[None, :], axis=1)
    scorer = 2 * pair_index + 1 - first_flag
    match_mask = (scorer[None, :] == doc_ids[:, None]).astype(jnp.int32)
    own_doc = jnp.sum(match_mask * doc_ids[None, :], axis=1)
    return (scorer, own_doc)


def rope_tables(length, head_dim):
    half_dim = head_dim // 2
    freq_ids = jnp.arange(half_dim, dtype=jnp.float32)
    inv_freq = jnp.exp(-(2.0 * freq_ids / head_dim) * jnp.log(jnp.float32(ROPE_BASE)))
    angles = jnp.arange(length, dtype=jnp.float32)[:, None] * inv_freq[None, :]
    cosine = jnp.concatenate([jnp.cos(angles), jnp.cos(angles)], axis=1)
    sine_table = jnp.concatenate([jnp.sin(angles), jnp.sin(angles)], axis=1)
    return (cosine, sine_table)


def rotate(heads, cosine, sine_table):
    widened = heads.astype(jnp.float32)
    half_dim = widened.shape[-1] // 2
    turned = jnp.concatenate([-widened[..., half_dim:], widened[..., :half_dim]], axis=-1)
    return (widened * cosine[:, None, :] + turned * sine_table[:, None, :]).astype(jnp.bfloat16)


def rms_norm(row_values, norm_gain):
    widened = row_values.astype(jnp.float32)
    inv_rms = lax.rsqrt(jnp.mean(widened * widened, axis=-1, keepdims=True) + EPSILON)
    return (widened * inv_rms * norm_gain.astype(jnp.float32)).astype(jnp.bfloat16)


def place_rows(values, dest_index, length):
    blank_rows = jnp.zeros((length,) + values.shape[1:], values.dtype)
    return blank_rows.at[dest_index].set(values, mode="drop")


def assemble(first_part, second_part, first_len):
    padded = jnp.concatenate([first_part, jnp.zeros_like(second_part)], axis=0)
    return lax.dynamic_update_slice(padded, second_part, (first_len, jnp.int32(0)))


def attention(projected, total_len, q_heads, kv_heads, head_dim):
    length = projected.shape[0]
    cosine, sine_table = rope_tables(length, head_dim)
    queries = rotate(
        projected[:, : q_heads * head_dim].reshape(length, q_heads, head_dim), cosine, sine_table
    )
    key_heads = rotate(
        projected[:, q_heads * head_dim : (q_heads + kv_heads) * head_dim].reshape(
            length, kv_heads, head_dim
        ),
        cosine,
        sine_table,
    )
    value_heads = projected[:, (q_heads + kv_heads) * head_dim :].reshape(
        length, kv_heads, head_dim
    )
    grouped = queries.reshape(length, kv_heads, q_heads // kv_heads, head_dim)
    block_length = min(BLOCK_ROWS, length)
    root_dim = jnp.sqrt(jnp.float32(head_dim))
    pieces = []
    for row_start in range(0, length, block_length):
        row_stop = row_start + block_length
        scores = (
            jnp.einsum(
                "qkgd,skd->kgqs",
                grouped[row_start:row_stop],
                key_heads[:row_stop],
                preferred_element_type=jnp.float32,
            )
            / root_dim
        )
        row_ids = jnp.arange(row_start, row_stop, dtype=jnp.int32)[:, None]
        col_ids = jnp.arange(row_stop, dtype=jnp.int32)[None, :]
        allowed = (col_ids <= row_ids) & (col_ids < total_len)
        scores = jnp.where(allowed, scores, -jnp.inf)
        largest = jnp.max(scores, axis=-1, keepdims=True)
        exponent = jnp.exp(scores - largest)
        probabilities = (exponent / jnp.sum(exponent, axis=-1, keepdims=True)).astype(jnp.bfloat16)
        mixture = jnp.einsum(
            "kgqs,skd->qkgd",
            probabilities,
            value_heads[:row_stop],
            preferred_element_type=jnp.float32,
        )
        live_rows = (jnp.arange(row_start, row_stop, dtype=jnp.int32) < total_len)[
            :, None, None, None
        ]
        mixture = jnp.where(live_rows, mixture, 0.0)
        pieces.append(mixture.astype(jnp.bfloat16).reshape(block_length, q_heads * head_dim))
    return jnp.concatenate(pieces, axis=0)


def shards(storage, row_doc, row_pos, doc_len, partner, norm_gain, qkv_weight, qkv_bias):
    doc_count = lax.axis_size("doc")
    me_index = lax.axis_index("doc")
    half_rows = HALF
    per_dest = half_rows // doc_count
    scorer, own_doc = pairing(partner)
    doc_ids = jnp.arange(doc_count, dtype=jnp.int32)
    first_doc = jnp.sum(jnp.where(doc_ids == me_index, own_doc, 0))
    second_doc = jnp.sum(jnp.where(doc_ids == first_doc, partner, 0))
    first_len = jnp.sum(jnp.where(doc_ids == first_doc, doc_len, 0))
    second_len = jnp.sum(jnp.where(doc_ids == second_doc, doc_len, 0))
    total_len = first_len + second_len
    stored = row_doc >= 0
    dest_scorer = jnp.sum(
        jnp.where(row_doc[:, None] == doc_ids[None, :], scorer[None, :], 0), axis=1
    )
    onehot = ((dest_scorer[:, None] == doc_ids[None, :]) & stored[:, None]).astype(jnp.int32)
    dest_rank = jnp.sum(jnp.cumsum(onehot, axis=0) * onehot, axis=1) - 1
    dest_index = jnp.where(stored, dest_scorer * per_dest + dest_rank, doc_count * per_dest)
    send_rows = place_rows(storage, dest_index, doc_count * per_dest).reshape(
        doc_count, per_dest, storage.shape[1]
    )
    send_pos = (
        jnp.full((doc_count * per_dest,), half_rows, jnp.int32)
        .at[dest_index]
        .set(row_pos, mode="drop")
    )
    send_pos = send_pos.reshape(doc_count, per_dest)
    got_rows, got_pos = (
        lax.all_to_all(send_rows, "doc", split_axis=0, concat_axis=0, tiled=True),
        lax.all_to_all(send_pos, "doc", split_axis=0, concat_axis=0, tiled=True),
    )
    own_rows = place_rows(
        got_rows.reshape(doc_count * per_dest, storage.shape[1]), got_pos.reshape(-1), half_rows
    )
    q_heads = HEADS // lax.axis_size("tp")
    kv_heads = KVH // lax.axis_size("tp")
    bias_wide = qkv_bias.astype(jnp.float32)
    other_rows = from_partner(own_rows, "doc", 0)
    both_full = lax.all_gather(
        jnp.concatenate([own_rows, other_rows], axis=0), "tp", axis=1, tiled=True
    )
    normed = rms_norm(both_full, norm_gain)
    full_weight = lax.all_gather(qkv_weight, "doc", axis=0, tiled=True)
    both_sum = jnp.dot(normed, full_weight, preferred_element_type=jnp.float32)
    both_proj = (both_sum + bias_wide).astype(jnp.bfloat16)
    projected = assemble(both_proj[:half_rows], both_proj[half_rows:], first_len)
    return attention(projected, total_len, q_heads, kv_heads, HD)


def solution(mesh):
    placed = (P("doc", "tp"), P("doc"), P("doc"), P(), P(), P(), P("doc", "tp"), P("tp"))
    return jax.shard_map(
        shards, mesh=mesh, in_specs=placed, out_specs=P("doc", "tp"), check_vma=False
    )
```

profile of v0, /device:TPU:1, one launch (start us, length us, event | category | flops | bytes accessed | tf_op | source)
XLA Modules:
  0.0 322.1 jit_solution(13756107359092494782)
XLA Ops:
  6.5 0.7 fusion.61
  7.2 0.7 broadcast_compare_fusion
  7.9 0.7 fusion.55
  8.9 0.7 iota_minimum_fusion
  9.7 0.7 add_subtract_fusion
  10.4 0.8 select_reduce_fusion
  11.2 1.2 reduce-window.20
  12.8 0.7 compare_select_fusion.1
  13.5 2.6 scatter_custom_fusion
  16.1 0.7 all_to_all.9
  16.8 13.2 %all-to-all-start = ((s32[64,1,8]{2,1,0:T(1,128)}), s32[64,1,8]{2,1,0:T(1,128)S(1)}, u32[]{:S(2)}, u32[]{:S(2)}) async-start(s32[64,1,8]{2,1,0:T(1,128)} %bitcast.4), calls=%async_computation | async-start | bytes 65536 | tf_op jit(solution)/shard_map/all_to_all | solution.py:151
  29.9 4.3 %scatter_custom_fusion.1 = bf16[512,896]{1,0:T(8,128)(2,1)} fusion(s32[512]{0:T(512)S(1)} %compare_select_fusion.1, bf16[512,896]{1,0:T(8,128)(2,1)} %param.8, bf16[]{:T(256)} %constant.24.clone.1), kind=kCustom, calls=%fused_computation.63 | custom fusion | bytes 918016 | tf_op jit(solution)/shard_map/scatter | solution.py:61
  34.2 5.1 %all-to-all-done = s32[64,1,8]{2,1,0:T(1,128)S(1)} async-done(((s32[64,1,8]{2,1,0:T(1,128)}), s32[64,1,8]{2,1,0:T(1,128)S(1)}, u32[]{:S(2)}, u32[]{:S(2)}) %all-to-all-start) | async-done | bytes 2080 | tf_op jit(solution)/shard_map/all_to_all | solution.py:151
  39.3 5.2 %all-to-all-start.1 = ((bf16[64,8,896]{2,1,0:T(8,128)(2,1)}), bf16[64,8,896]{2,1,0:T(8,128)(2,1)S(1)}, u32[]{:S(2)}, u32[]{:S(2)}) async-start(bf16[64,8,896]{2,1,0:T(8,128)(2,1)} %bitcast.6), calls=%async_computation.1 | async-start | bytes 1835008 | tf_op jit(solution)/shard_map/all_to_all | solution.py:150
  44.6 0.6 broadcast.173
  45.1 0.8 reduce.10
  46.0 23.8 %all-to-all-done.1 = bf16[64,8,896]{2,1,0:T(8,128)(2,1)S(1)} async-done(((bf16[64,8,896]{2,1,0:T(8,128)(2,1)}), bf16[64,8,896]{2,1,0:T(8,128)(2,1)S(1)}, u32[]{:S(2)}, u32[]{:S(2)}) %all-to-all-start.1) | async-done | bytes 917536 | tf_op jit(solution)/shard_map/all_to_all | solution.py:150
  69.8 2.9 scatter_custom_fusion.2
  72.8 1.3 collective-permute-start
  74.1 2.1 collective-permute-done
  76.2 1.4 pad_maximum_fusion
  77.8 0.5 all-gather.5.cloned.1.call-update
  78.5 0.6 fusion.52
  79.1 1.2 fusion.51
  80.4 1.8 fusion.53
  85.6 1.9 fusion.38
  87.6 63.3 %all-gather.3.cloned.1.call-done = bf16[1024,3584]{1,0:T(8,128)(2,1)} async-done(((bf16[1024,896]{1,0:T(8,128)(2,1)}), bf16[1024,3584]{1,0:T(8,128)(2,1)}) %all-gather.3.cloned.1.call-update) | async-done | bytes 7340048 | tf_op jit(solution)/shard_map/all_gather | solution.py:160
  150.9 4.6 %fusion = f32[1024]{0:T(1024)S(1)} fusion(bf16[1024,3584]{1,0:T(8,128)(2,1)} %all-gather.3.cloned.1.call-done), kind=kLoop, calls=%fused_computation.5 | loop fusion | flops 11009024 | bytes 7344128 | tf_op jit(solution)/shard_map/reduce_sum | solution.py:55
  155.5 82.3 %all-gather.5.cloned.1.call-done = bf16[3584,1152]{1,0:T(8,128)(2,1)} async-done(((bf16[56,1152]{1,0:T(8,128)(2,1)}), bf16[3584,1152]{1,0:T(8,128)(2,1)}) %all-gather.5.cloned.1.call-update) | async-done | bytes 8257552 | tf_op jit(solution)/shard_map/all_gather | solution.py:164
  237.8 15.6 %broadcast_select_fusion = (bf16[1024,1152]{1,0:T(8,128)(2,1)}, bf16[1024,1152]{1,0:T(8,128)(2,1)S(1)}) fusion(pred[1024]{0:T(1024)(128)(4,1)S(1)} %copy-done.5, f32[1152]{0:T(1024)S(1)} %convert_element_type.67, bf16[3584,1152]{1,0:T(8,128)(2,1)} %all-gather.5.cloned.1.call-done, bf16[1024,3584]{1,0:T(8,128)(2,1)} %all-gather.3.cloned.1.call-done, ...), kind=kOutput, calls=%fused_computation.31 | convolution fusion | flops 8473935872 | bytes 20340224 | tf_op jit(solution)/shard_map/dot_general | solution.py:165
  253.4 6.3 %dynamic_update_slice.3 = bf16[1024,1152]{1,0:T(8,128)(2,1)} dynamic-update-slice(bf16[1024,1152]{1,0:T(8,128)(2,1)} %get-tuple-element.18, bf16[512,1152]{1,0:T(8,128)(2,1)S(1)} %slice.64, s32[]{:T(128)S(6)} %select_n.63, s32[]{:T(128)} %constant.20.clone.1) | dynamic-update-slice | bytes 2359300 | tf_op jit(solution)/shard_map/dynamic_update_slice | solution.py:66
  259.8 1.0 convert_bitcast_fusion
  260.8 3.6 %slice_convert_fusion = f32[1024,896]{1,0:T(8,128)} fusion(bf16[1024,1152]{1,0:T(8,128)(2,1)} %dynamic_update_slice.3), kind=kLoop, calls=%fused_computation.34 | loop fusion | flops 917504 | bytes 5505024 | tf_op jit(solution)/shard_map/convert_element_type | solution.py:47
  264.5 5.1 %copy.47 = f32[1024,896]{0,1:T(8,128)} copy(f32[1024,896]{1,0:T(8,128)} %slice_convert_fusion) | data formatting | bytes 7340032 | tf_op jit(solution)/shard_map/convert_element_type | solution.py:47
  269.6 5.0 %copy.48 = f32[1024,7,128]{2,0,1:T(8,128)} copy(f32[1024,7,128]{0,2,1:T(8,128)} %bitcast.104) | data formatting | bytes 7340032 | tf_op jit(solution)/shard_map/convert_element_type | solution.py:47
  274.6 4.4 %slice_negate_fusion = (f32[1024,7,64]{2,0,1:T(8,128)S(1)}, f32[1024,7,64]{2,0,1:T(8,128)S(1)}) fusion(f32[1024,7,128]{2,0,1:T(8,128)} %copy.48), kind=kLoop, calls=%fused_computation.24 | loop fusion | flops 458752 | bytes 7340032 | tf_op jit(solution)/shard_map/neg | solution.py:49
  279.0 1.6 fusion.35
  280.6 0.5 copy-done
  281.1 1.1 fusion.16
  282.3 1.3 fusion.12
  283.5 1.5 fusion.11
  285.1 4.0 %fusion.22 = bf16[1,128,7,512]{3,1,2,0:T(8,128)(2,1)} fusion(f32[7,512]{1,0:T(8,128)S(1)} %fusion.11, f32[7,512]{1,0:T(8,128)S(1)} %get-tuple-element.22, f32[512,512,7]{1,0,2:T(8,128)S(1)} %get-tuple-element.23, pred[512,512]{0,1:T(8,128)(4,1)S(1)} %fusion.27, pred[512]{0:T(512)(128)(4,1)S(1)} %get-tuple-element.24, bf16[1024,1152]{1,0:T(8,128)(2,1)} %dynamic_update_slice.3), kind=kOutput, calls=%fused_computation.40 | convolution fusion | flops 479854592 | bytes 8679936 | tf_op jit(solution)/shard_map/kgqs,skd->qkgd/dot_general | solution.py:107
  289.1 1.5 copy.55
  290.7 6.8 %fusion.4 = (f32[7,512]{1,0:T(8,128)S(1)}, f32[1024,512,7]{1,0,2:T(8,128)}) fusion(pred[512,1024]{0,1:T(8,128)(4,1)S(1)} %fusion.20, bf16[1024,7,128]{2,0,1:T(8,128)(2,1)S(1)} %fusion.16, bf16[1024,128]{1,0:T(8,128)(2,1)S(1)} %get-tuple-element.9), kind=kOutput, calls=%fused_computation.12 | convolution fusion | flops 950530560 | bytes 16398336 | tf_op jit(solution)/shard_map/qkgd,skd->kgqs/dot_general | solution.py:92
  297.4 8.2 %fusion.3 = f32[7,512]{1,0:T(8,128)S(1)} fusion(f32[1024,512,7]{1,0,2:T(8,128)} %get-tuple-element.21, f32[7,512]{1,0:T(8,128)S(1)} %get-tuple-element.20, pred[512,1024]{0,1:T(8,128)(4,1)S(1)} %fusion.20), kind=kLoop, calls=%fused_computation.11 | loop fusion | flops 14676480 | bytes 15233024 | tf_op jit(solution)/shard_map/reduce_sum | solution.py:106
  305.6 7.7 %fusion.21 = bf16[1,128,7,512]{3,1,2,0:T(8,128)(2,1)S(1)} fusion(f32[7,512]{1,0:T(8,128)S(1)} %fusion.3, f32[7,512]{1,0:T(8,128)S(1)} %get-tuple-element.20, f32[1024,512,7]{1,0,2:T(8,128)} %get-tuple-element.21, pred[512,1024]{0,1:T(8,128)(4,1)S(1)} %fusion.20, pred[512]{0:T(512)(128)(4,1)S(1)} %get-tuple-element.25, ...), kind=kOutput, calls=%fused_computation.38 | convolution fusion | flops 958791680 | bytes 16413184 | tf_op jit(solution)/shard_map/kgqs,skd->qkgd/dot_general | solution.py:107
  313.3 0.6 copy.56
  313.9 1.4 pad_maximum_fusion.1
  (37 shorter events, 2.3 us)
Async XLA Ops:
  16.8 22.5 %all-to-all-start = ((s32[64,1,8]{2,1,0:T(1,128)}), s32[64,1,8]{2,1,0:T(1,128)S(1)}, u32[]{:S(2)}, u32[]{:S(2)}) async-start(s32[64,1,8]{2,1,0:T(1,128)} %bitcast.4), calls=%async_computation | async-start | bytes 65536 | tf_op jit(solution)/shard_map/all_to_all | solution.py:151
  39.3 30.5 %all-to-all-start.1 = ((bf16[64,8,896]{2,1,0:T(8,128)(2,1)}), bf16[64,8,896]{2,1,0:T(8,128)(2,1)S(1)}, u32[]{:S(2)}, u32[]{:S(2)}) async-start(bf16[64,8,896]{2,1,0:T(8,128)(2,1)} %bitcast.6), calls=%async_computation.1 | async-start | bytes 1835008 | tf_op jit(solution)/shard_map/all_to_all | solution.py:150
  44.5 106.4 %all-gather.3.cloned.1.call-start = ((), (), s32[]{:S(2)}) async-start(), calls=%async_computation.2 | async-start | bytes 9175040 | tf_op jit(solution)/shard_map/all_gather | solution.py:160
  69.8 8.5 %copy-start.1 = (bf16[3584]{0:T(1024)(128)(2,1)S(1)}, bf16[3584]{0:T(1024)(128)(2,1)}, u32[]{:S(2)}) copy-start(bf16[3584]{0:T(1024)(128)(2,1)} %param.13) | copy-start | bytes 21508
  69.8 8.6 %copy-start.2 = (bf16[1152]{0:T(1024)(128)(2,1)S(1)}, bf16[1152]{0:T(1024)(128)(2,1)}, u32[]{:S(2)}) copy-start(bf16[1152]{0:T(1024)(128)(2,1)} %param.15) | copy-start | bytes 6916
  69.8 9.3 %copy-start.4 = (s32[64]{0:T(128)S(1)}, s32[64]{0:T(128)}, u32[]{:S(2)}) copy-start(s32[64]{0:T(128)} %param.12) | copy-start | bytes 772
  69.8 10.6 %copy-start.3 = (s32[64]{0:T(128)S(1)}, s32[64]{0:T(128)}, u32[]{:S(2)}) copy-start(s32[64]{0:T(128)} %param.11) | copy-start | bytes 772
  72.8 3.4 %collective-permute-start = (bf16[512,896]{1,0:T(8,128)(2,1)S(1)}, bf16[512,896]{1,0:T(8,128)(2,1)S(1)}, u32[]{:S(2)}, u32[]{:S(2)}) collective-permute-start(bf16[512,896]{1,0:T(8,128)(2,1)S(1)} %scatter_custom_fusion.2), channel_id=1, source_target_pairs={{0,4},{4,0},{8,12},{12,8},{16,20},{20,16},{24,28},{28,24},{32,36},... | collective-permute-start | bytes 2752520 | tf_op jit(solution)/shard_map/ppermute | solution.py:20
  77.6 160.2 %all-gather.5.cloned.1.call-start = ((), (), s32[]{:S(2)}) async-start(), calls=%async_computation.3 | async-start | bytes 8386560 | tf_op jit(solution)/shard_map/all_gather | solution.py:164
  87.6 150.2 %copy-start.5 = (pred[1024]{0:T(1024)(128)(4,1)S(1)}, pred[1024]{0:T(1024)(128)(4,1)}, u32[]{:S(2)}) copy-start(pred[1024]{0:T(1024)(128)(4,1)} %constant.16.clone.1) | copy-start | bytes 3076
  279.0 2.1 copy-start
Sparse Core Ops, SparseCore 0:
  77.7 73.1 all-gather.2
  153.6 84.1 all-gather.4
where the time goes:
time: 323 us; the launch traced here: 322 us
  waiting for transfers between devices  177 us (55%)
  other arithmetic  42.6 us (13%)
  matrix products  35.3 us (11%)
  local copies, waits for them, and re-layouts  30.7 us (10%)
  starting transfers between devices  19.9 us (6%)
  between operations  16.5 us (5%)
    all_gather x1, waiting for transfers between devices, shards(): full_weight = lax.all_gather(qkv_weight, 'doc', axis=0, tiled=True)  82.3 us
    all_gather x1, waiting for transfers between devices, shards(): lax.all_gather(jnp.concatenate([own_rows, other_rows], axis=0), 'tp', axi...  63.3 us
    all_to_all x1, waiting for transfers between devices, shards(): lax.all_to_all(send_rows, 'doc', split_axis=0, concat_axis=0, tiled=True)  23.8 us
    dot_general x1, matrix products, shards(): both_sum = jnp.dot(normed, full_weight, preferred_element_type=jnp.float32)  15.6 us
    all_to_all x1, starting transfers between devices, shards(): lax.all_to_all(send_pos, 'doc', split_axis=0, concat_axis=0, tiled=True)  13.2 us
    dot_general x2, matrix products, attention(): jnp.einsum('kgqs,skd->qkgd', probabilities, value_heads[:row_stop], prefe...  11.7 us
    convert_element_type x2, local copies, waits for them, and re-layouts, rotate(): widened = heads.astype(jnp.float32)  10.1 us
    reduce_sum x2, other arithmetic, attention(): jnp.sum(exponent, axis=-1, keepdims=True)  9.7 us
  transfers between devices with their start and end apart: 5, of which 5 were waited for; matrix products, arithmetic and copies ran while one was open for 5% of the time, Pallas kernels for 0%

commit v1 on v0

--- a/solution.py
+++ b/solution.py
@@ -119,8 +119,10 @@
 
 
 def shards(storage, row_doc, row_pos, doc_len, partner, norm_gain, qkv_weight, qkv_bias):
-    doc_count = lax.axis_size("doc")
-    me_index = lax.axis_index("doc")
+    pair_count = lax.axis_size("pair")
+    doc_count = 2 * pair_count
+    core = lax.axis_index("core")
+    me_index = lax.axis_index("pair") * 2 + core
     half_rows = HALF
     per_dest = half_rows // doc_count
     scorer, own_doc = pairing(partner)
@@ -146,9 +148,10 @@
         .set(row_pos, mode="drop")
     )
     send_pos = send_pos.reshape(doc_count, per_dest)
+    doc_axes = ("pair", "core")
     got_rows, got_pos = (
-        lax.all_to_all(send_rows, "doc", split_axis=0, concat_axis=0, tiled=True),
-        lax.all_to_all(send_pos, "doc", split_axis=0, concat_axis=0, tiled=True),
+        lax.all_to_all(send_rows, doc_axes, split_axis=0, concat_axis=0, tiled=True),
+        lax.all_to_all(send_pos, doc_axes, split_axis=0, concat_axis=0, tiled=True),
     )
     own_rows = place_rows(
         got_rows.reshape(doc_count * per_dest, storage.shape[1]), got_pos.reshape(-1), half_rows
@@ -156,20 +159,28 @@
     q_heads = HEADS // lax.axis_size("tp")
     kv_heads = KVH // lax.axis_size("tp")
     bias_wide = qkv_bias.astype(jnp.float32)
-    other_rows = from_partner(own_rows, "doc", 0)
-    both_full = lax.all_gather(
-        jnp.concatenate([own_rows, other_rows], axis=0), "tp", axis=1, tiled=True
-    )
-    normed = rms_norm(both_full, norm_gain)
-    full_weight = lax.all_gather(qkv_weight, "doc", axis=0, tiled=True)
-    both_sum = jnp.dot(normed, full_weight, preferred_element_type=jnp.float32)
-    both_proj = (both_sum + bias_wide).astype(jnp.bfloat16)
-    projected = assemble(both_proj[:half_rows], both_proj[half_rows:], first_len)
+    own_full = lax.all_gather(own_rows, "tp", axis=1, tiled=True)
+    normed = rms_norm(own_full, norm_gain)
+    mine = lax.all_gather(qkv_weight, "pair", axis=0, tiled=False)
+    theirs = from_partner(mine, "core", 0)
+    is_first = core == 0
+    low = jnp.where(is_first, mine, theirs)
+    high = jnp.where(is_first, theirs, mine)
+    full_weight = jnp.stack([low, high], axis=1).reshape(-1, qkv_weight.shape[1])
+    own_sum = jnp.dot(normed, full_weight, preferred_element_type=jnp.float32)
+    own_proj = (own_sum + bias_wide).astype(jnp.bfloat16)
+    other_proj = from_partner(own_proj, "core", 0)
+    projected = assemble(own_proj, other_proj, first_len)
     return attention(projected, total_len, q_heads, kv_heads, HD)
 
 
 def solution(mesh):
-    placed = (P("doc", "tp"), P("doc"), P("doc"), P(), P(), P(), P("doc", "tp"), P("tp"))
+    doc_count, tp_count = mesh.shape["doc"], mesh.shape["tp"]
+    split = jax.sharding.Mesh(
+        mesh.devices.reshape(doc_count // 2, 2, tp_count), ("pair", "core", "tp")
+    )
+    rows = ("pair", "core")
+    placed = (P(rows, "tp"), P(rows), P(rows), P(), P(), P(), P(rows, "tp"), P("tp"))
     return jax.shard_map(
-        shards, mesh=mesh, in_specs=placed, out_specs=P("doc", "tp"), check_vma=False
+        shards, mesh=split, in_specs=placed, out_specs=P(rows, "tp"), check_vma=False
     )

time: 323 us -> 250 us (0.77)
  waiting for transfers between devices: 177 us -> 91.9 us
  other arithmetic: 42.6 us -> 49.6 us
  local copies, waits for them, and re-layouts: 30.7 us -> 36.4 us
  matrix products: 35.3 us -> 30.8 us
  starting transfers between devices: 19.9 us -> 23.3 us
    all_gather x2, waiting for transfers between devices: 146 us -> 61.3 us  [the longest x1 42.4 us: shards(): own_full = lax.all_gather(own_rows, 'tp', axis=1, tiled=True)]
    another operation x5 -> x7, other arithmetic: 2.1 us -> 13.4 us  [the longest x2 11.3 us: shards(): jnp.stack([low, high], axis=1).reshape(-1, qkv_weight.shape[1])]
    dot_general x1, matrix products: 15.6 us -> 10.4 us  [shards(): own_sum = jnp.dot(normed, full_weight, preferred_element_type=jnp.float32)]
    ppermute x1 -> x2, starting transfers between devices: 1.32 us -> 4.97 us  [from_partner(): return lax.ppermute(value, axis, pairs)]
  transfers between devices with their start and end apart: 5 -> 6, of which waited for: 5 -> 4; matrix products, arithmetic and copies ran while one was open for 5% -> 12% of each run, Pallas kernels for 0% -> 0%
where the time goes in v1:
time: 250 us; the launch traced here: 249 us
  waiting for transfers between devices  91.9 us (37%)
  other arithmetic  49.6 us (20%)
  local copies, waits for them, and re-layouts  36.4 us (15%)
  matrix products  30.8 us (12%)
  starting transfers between devices  23.3 us (9%)
  between operations  16.8 us (7%)
    all_gather x1, waiting for transfers between devices, shards(): own_full = lax.all_gather(own_rows, 'tp', axis=1, tiled=True)  42.4 us
    all_to_all x1, waiting for transfers between devices, shards(): lax.all_to_all(send_rows, doc_axes, split_axis=0, concat_axis=0, tiled=True)  24.7 us
    all_gather x1, waiting for transfers between devices, shards(): mine = lax.all_gather(qkv_weight, 'pair', axis=0, tiled=False)  18.9 us
    all_to_all x1, starting transfers between devices, shards(): lax.all_to_all(send_pos, doc_axes, split_axis=0, concat_axis=0, tiled=True)  13.2 us
    dot_general x2, matrix products, attention(): jnp.einsum('kgqs,skd->qkgd', probabilities, value_heads[:row_stop], prefe...  12.6 us
    another operation x2, other arithmetic, shards(): jnp.stack([low, high], axis=1).reshape(-1, qkv_weight.shape[1])  11.3 us
    dot_general x1, matrix products, shards(): own_sum = jnp.dot(normed, full_weight, preferred_element_type=jnp.float32)  10.4 us
    convert_element_type x2, local copies, waits for them, and re-layouts, rotate(): widened = heads.astype(jnp.float32)  10.1 us
  transfers between devices with their start and end apart: 6, of which 4 were waited for; matrix products, arithmetic and copies ran while one was open for 12% of the time, Pallas kernels for 0%

profile of v1, /device:TPU:1, one launch (start us, length us, event | category | flops | bytes accessed | tf_op | source)
XLA Modules:
  0.0 248.7 jit_solution(14632437046160385297)
XLA Ops:
  6.5 0.7 all-gather.6.cloned.1.call-update
  7.3 0.7 fusion.59
  8.2 0.7 iota_minimum_fusion
  9.1 0.7 add_subtract_fusion
  9.7 0.8 select_reduce_fusion
  10.5 0.7 fusion.65
  11.2 1.2 reduce-window.20
  12.7 0.7 broadcast_compare_fusion
  13.5 0.7 compare_select_fusion.1
  14.2 2.6 %scatter_custom_fusion = s32[512]{0:T(512)S(1)} fusion(s32[512]{0:T(512)S(1)} %compare_select_fusion.1, s32[512]{0:T(512)} %param.10, s32[]{:T(128)} %constant.27.clone.1), kind=kCustom, calls=%fused_computation.99 | custom fusion | bytes 2560 | tf_op jit(solution)/shard_map/scatter | solution.py:148
  16.8 0.7 all_to_all.9
  17.5 13.2 %all-to-all-start = ((s32[64,1,8]{2,1,0:T(1,128)}), s32[64,1,8]{2,1,0:T(1,128)S(1)}, u32[]{:S(2)}, u32[]{:S(2)}) async-start(s32[64,1,8]{2,1,0:T(1,128)} %bitcast.4), calls=%async_computation | async-start | bytes 65536 | tf_op jit(solution)/shard_map/all_to_all | solution.py:154
  30.7 4.3 %scatter_custom_fusion.1 = bf16[512,896]{1,0:T(8,128)(2,1)} fusion(s32[512]{0:T(512)S(1)} %compare_select_fusion.1, bf16[512,896]{1,0:T(8,128)(2,1)} %param.8, bf16[]{:T(256)} %constant.17.clone.1), kind=kCustom, calls=%fused_computation.65 | custom fusion | bytes 918016 | tf_op jit(solution)/shard_map/scatter | solution.py:61
  34.9 5.2 %all-to-all-done = s32[64,1,8]{2,1,0:T(1,128)S(1)} async-done(((s32[64,1,8]{2,1,0:T(1,128)}), s32[64,1,8]{2,1,0:T(1,128)S(1)}, u32[]{:S(2)}, u32[]{:S(2)}) %all-to-all-start) | async-done | bytes 2080 | tf_op jit(solution)/shard_map/all_to_all | solution.py:154
  40.1 5.1 %all-to-all-start.1 = ((bf16[64,8,896]{2,1,0:T(8,128)(2,1)}), bf16[64,8,896]{2,1,0:T(8,128)(2,1)S(1)}, u32[]{:S(2)}, u32[]{:S(2)}) async-start(bf16[64,8,896]{2,1,0:T(8,128)(2,1)} %bitcast.6), calls=%async_computation.1 | async-start | bytes 1835008 | tf_op jit(solution)/shard_map/all_to_all | solution.py:153
  45.8 0.7 reduce.10
  46.7 24.7 %all-to-all-done.1 = bf16[64,8,896]{2,1,0:T(8,128)(2,1)S(1)} async-done(((bf16[64,8,896]{2,1,0:T(8,128)(2,1)}), bf16[64,8,896]{2,1,0:T(8,128)(2,1)S(1)}, u32[]{:S(2)}, u32[]{:S(2)}) %all-to-all-start.1) | async-done | bytes 917536 | tf_op jit(solution)/shard_map/all_to_all | solution.py:153
  71.4 3.6 %scatter_custom_fusion.2 = bf16[512,896]{1,0:T(8,128)(2,1)} fusion(s32[512]{0:T(512)S(1)} %bitcast.119, bf16[64,8,896]{2,1,0:T(8,128)(2,1)S(1)} %all-to-all-done.1, bf16[]{:T(256)} %constant.17.clone.1), kind=kCustom, calls=%fused_computation.49 | custom fusion | bytes 1835010 | tf_op jit(solution)/shard_map/scatter | solution.py:61
  75.0 18.9 %all-gather.6.cloned.1.call-done = bf16[1792,1152]{1,0:T(8,128)(2,1)} async-done(((bf16[56,1152]{1,0:T(8,128)(2,1)}), bf16[1792,1152]{1,0:T(8,128)(2,1)}) %all-gather.6.cloned.1.call-update) | async-done | bytes 4128784 | tf_op jit(solution)/shard_map/all_gather | solution.py:164
  94.0 4.2 %collective-permute-start = (bf16[32,56,1152]{2,1,0:T(8,128)(2,1)}, bf16[32,56,1152]{2,1,0:T(8,128)(2,1)}, u32[]{:S(2)}, u32[]{:S(2)}) collective-permute-start(bf16[32,56,1152]{2,1,0:T(8,128)(2,1)} %bitcast.114), channel_id=1, source_target_pairs={{0,4},{4,0},{1,5},{5,1},{2,6},{6,2},{3,7},{7,3},{8,12},{12,8},{9,1... | collective-permute-start | bytes 12386312 | tf_op jit(solution)/shard_map/ppermute | solution.py:20
  98.4 0.7 fusion.56
  99.1 1.3 fusion.55
  100.4 42.4 %all-gather.4.cloned.1.call-done = bf16[512,3584]{1,0:T(8,128)(2,1)} async-done(((bf16[512,896]{1,0:T(8,128)(2,1)}), bf16[512,3584]{1,0:T(8,128)(2,1)}) %all-gather.4.cloned.1.call-update) | async-done | bytes 3670032 | tf_op jit(solution)/shard_map/all_gather | solution.py:162
  142.8 2.8 %fusion.2 = f32[512]{0:T(512)S(1)} fusion(bf16[512,3584]{1,0:T(8,128)(2,1)} %all-gather.4.cloned.1.call-done), kind=kLoop, calls=%fused_computation.11 | loop fusion | flops 5504512 | bytes 3672064 | tf_op jit(solution)/shard_map/reduce_sum | solution.py:55
  145.6 5.1 %select_bitcast_fusion.1 = (bf16[32,1,56,1152]{3,2,1,0:T(8,128)(2,1)S(1)}, bf16[32,1,56,1152]{3,2,1,0:T(8,128)(2,1)}) fusion(bf16[32,56,1152]{2,1,0:T(8,128)(2,1)} %bitcast.115, bf16[32,56,1152]{2,1,0:T(8,128)(2,1)} %collective-permute-done, pred[]{:T(512)S(6)} %eq.110), kind=kLoop, calls=%fused_computation.22 | loop fusion | flops 4128768 | bytes 16515073 | tf_op jit(solution)/shard_map/stack | solution.py:169
  150.7 6.2 %pad_maximum_fusion = bf16[32,2,56,1152]{3,2,1,0:T(8,128)(2,1)} fusion(bf16[32,1,56,1152]{3,2,1,0:T(8,128)(2,1)} %get-tuple-element.8, bf16[32,1,56,1152]{3,2,1,0:T(8,128)(2,1)S(1)} %get-tuple-element.7), kind=kLoop, calls=%fused_computation.10 | loop fusion | flops 4128768 | bytes 16515072 | tf_op jit(solution)/shard_map/stack | solution.py:169
  156.9 10.4 %fusion.21 = bf16[512,1152]{1,0:T(8,128)(2,1)} fusion(bf16[3584,1152]{1,0:T(8,128)(2,1)} %bitcast.113, bf16[512,3584]{1,0:T(8,128)(2,1)} %all-gather.4.cloned.1.call-done, f32[3584]{0:T(1024)S(1)} %convert_element_type.65, f32[512]{0:T(512)S(1)} %add_rsqrt_fusion, f32[1152]{0:T(1024)S(1)} %convert_element_type.67), kind=kOutput, calls=%fused_computation.34 | convolution fusion | flops 4236378112 | bytes 13128192 | tf_op jit(solution)/shard_map/dot_general | solution.py:170
  167.3 0.7 collective-permute-start.1
  168.1 2.0 fusion.57
  173.7 2.8 %fusion.42 = (f32[1024,64]{1,0:T(8,128)}, f32[1024,64]{1,0:T(8,128)}) fusion(f32[64]{0:T(128)S(1)} %multiply_exponential_fusion), kind=kLoop, calls=%fused_computation.63 | loop fusion | flops 65536 | bytes 524544 | tf_op jit(solution)/shard_map/cos | solution.py:41
  176.6 1.4 concatenate.23
  178.0 7.4 %dynamic_update_slice.3 = bf16[1024,1152]{1,0:T(8,128)(2,1)S(1)} dynamic-update-slice(bf16[1024,1152]{1,0:T(8,128)(2,1)S(1)} %concatenate.23, bf16[512,1152]{1,0:T(8,128)(2,1)} %collective-permute-done.1, s32[]{:T(128)S(6)} %select_n.78, s32[]{:T(128)} %constant.24.clone.1) | dynamic-update-slice | bytes 2359300 | tf_op jit(solution)/shard_map/dynamic_update_slice | solution.py:66
  185.5 2.2 slice_convert_fusion
  187.7 1.1 fusion.40
  188.9 5.0 %copy.50 = f32[1024,896]{0,1:T(8,128)} copy(f32[1024,896]{1,0:T(8,128)} %slice_convert_fusion) | data formatting | bytes 7340032 | tf_op jit(solution)/shard_map/convert_element_type | solution.py:47
  193.9 5.0 %copy.51 = f32[1024,7,128]{2,0,1:T(8,128)} copy(f32[1024,7,128]{0,2,1:T(8,128)} %bitcast.112) | data formatting | bytes 7340032 | tf_op jit(solution)/shard_map/convert_element_type | solution.py:47
  199.0 4.5 %slice_negate_fusion = (f32[1024,7,64]{2,0,1:T(8,128)S(1)}, f32[1024,7,64]{2,0,1:T(8,128)S(1)}) fusion(f32[1024,7,128]{2,0,1:T(8,128)} %copy.51), kind=kLoop, calls=%fused_computation.24 | loop fusion | flops 458752 | bytes 7340032 | tf_op jit(solution)/shard_map/neg | solution.py:49
  204.0 1.5 copy-done
  205.5 1.1 fusion.12
  206.6 1.3 fusion.8
  207.9 1.5 fusion.7
  209.4 4.0 %fusion.26 = bf16[1,128,7,512]{3,1,2,0:T(8,128)(2,1)} fusion(f32[7,512]{1,0:T(8,128)S(1)} %fusion.7, f32[7,512]{1,0:T(8,128)S(1)} %get-tuple-element.22, f32[512,512,7]{1,0,2:T(8,128)S(1)} %get-tuple-element.23, pred[512,512]{0,1:T(8,128)(4,1)S(1)} %fusion.31, pred[512]{0:T(512)(128)(4,1)S(1)} %get-tuple-element.24, bf16[1024,1152]{1,0:T(8,128)(2,1)} %copy-done.1), kind=kOutput, calls=%fused_computation.42 | convolution fusion | flops 479854592 | bytes 8679936 | tf_op jit(solution)/shard_map/kgqs,skd->qkgd/dot_general | solution.py:107
  213.5 2.2 copy.58
  215.7 6.5 %fusion.1 = (f32[7,512]{1,0:T(8,128)S(1)}, f32[1024,512,7]{1,0,2:T(8,128)}) fusion(pred[512,1024]{0,1:T(8,128)(4,1)S(1)} %fusion.24, bf16[1024,7,128]{2,0,1:T(8,128)(2,1)S(1)} %fusion.12, bf16[1024,128]{1,0:T(8,128)(2,1)S(1)} %get-tuple-element.11), kind=kOutput, calls=%fused_computation.7 | convolution fusion | flops 950530560 | bytes 16398336 | tf_op jit(solution)/shard_map/qkgd,skd->kgqs/dot_general | solution.py:92
  222.2 8.2 %fusion = f32[7,512]{1,0:T(8,128)S(1)} fusion(f32[1024,512,7]{1,0,2:T(8,128)} %get-tuple-element.21, f32[7,512]{1,0:T(8,128)S(1)} %get-tuple-element.20, pred[512,1024]{0,1:T(8,128)(4,1)S(1)} %fusion.24), kind=kLoop, calls=%fused_computation.6 | loop fusion | flops 14676480 | bytes 15233024 | tf_op jit(solution)/shard_map/reduce_sum | solution.py:106
  230.4 8.5 %fusion.25 = bf16[1,128,7,512]{3,1,2,0:T(8,128)(2,1)} fusion(f32[7,512]{1,0:T(8,128)S(1)} %fusion, f32[7,512]{1,0:T(8,128)S(1)} %get-tuple-element.20, f32[1024,512,7]{1,0,2:T(8,128)} %get-tuple-element.21, pred[512,1024]{0,1:T(8,128)(4,1)S(1)} %fusion.24, pred[512]{0:T(512)(128)(4,1)S(1)} %get-tuple-element.25, bf16[1024,1152]{1,0:T(8,128)(2,1)} %copy-done.1), kind=kOutput, calls=%fused_computation.40 | convolution fusion | flops 958791680 | bytes 16413184 | tf_op jit(solution)/shard_map/kgqs,skd->qkgd/dot_general | solution.py:107
  238.9 1.5 copy.59
  240.4 1.4 pad_maximum_fusion.1
  (50 shorter events, 2.8 us)
Async XLA Ops:
  6.5 92.5 %copy-start.10 = (s32[64]{0:T(128)S(1)}, s32[64]{0:T(128)}, u32[]{:S(2)}) copy-start(s32[64]{0:T(128)} %param.12) | copy-start | bytes 772
  6.5 91.7 %copy-start.7 = (bf16[3584]{0:T(1024)(128)(2,1)S(1)}, bf16[3584]{0:T(1024)(128)(2,1)}, u32[]{:S(2)}) copy-start(bf16[3584]{0:T(1024)(128)(2,1)} %param.13) | copy-start | bytes 21508
  6.5 91.7 %copy-start.8 = (bf16[1152]{0:T(1024)(128)(2,1)S(1)}, bf16[1152]{0:T(1024)(128)(2,1)}, u32[]{:S(2)}) copy-start(bf16[1152]{0:T(1024)(128)(2,1)} %param.15) | copy-start | bytes 6916
  6.5 87.4 %all-gather.6.cloned.1.call-start = ((), (), s32[]{:S(2)}) async-start(), calls=%async_computation.3 | async-start | bytes 4257792 | tf_op jit(solution)/shard_map/all_gather | solution.py:164
  17.5 22.6 %all-to-all-start = ((s32[64,1,8]{2,1,0:T(1,128)}), s32[64,1,8]{2,1,0:T(1,128)S(1)}, u32[]{:S(2)}, u32[]{:S(2)}) async-start(s32[64,1,8]{2,1,0:T(1,128)} %bitcast.4), calls=%async_computation | async-start | bytes 65536 | tf_op jit(solution)/shard_map/all_to_all | solution.py:154
  40.1 31.3 %all-to-all-start.1 = ((bf16[64,8,896]{2,1,0:T(8,128)(2,1)}), bf16[64,8,896]{2,1,0:T(8,128)(2,1)S(1)}, u32[]{:S(2)}, u32[]{:S(2)}) async-start(bf16[64,8,896]{2,1,0:T(8,128)(2,1)} %bitcast.6), calls=%async_computation.1 | async-start | bytes 1835008 | tf_op jit(solution)/shard_map/all_to_all | solution.py:153
  45.2 97.5 %all-gather.4.cloned.1.call-start = ((), (), s32[]{:S(2)}) async-start(), calls=%async_computation.2 | async-start | bytes 4587520 | tf_op jit(solution)/shard_map/all_gather | solution.py:162
  94.0 51.6 %collective-permute-start = (bf16[32,56,1152]{2,1,0:T(8,128)(2,1)}, bf16[32,56,1152]{2,1,0:T(8,128)(2,1)}, u32[]{:S(2)}, u32[]{:S(2)}) collective-permute-start(bf16[32,56,1152]{2,1,0:T(8,128)(2,1)} %bitcast.114), channel_id=1, source_target_pairs={{0,4},{4,0},{1,5},{5,1},{2,6},{6,2},{3,7},{7,3},{8,12},{12,8},{9,1... | collective-permute-start | bytes 12386312 | tf_op jit(solution)/shard_map/ppermute | solution.py:20
  156.9 11.2 %copy-start.9 = (s32[64]{0:T(128)S(1)}, s32[64]{0:T(128)}, u32[]{:S(2)}) copy-start(s32[64]{0:T(128)} %param.11) | copy-start | bytes 772
  167.3 10.7 %collective-permute-start.1 = (bf16[512,1152]{1,0:T(8,128)(2,1)}, bf16[512,1152]{1,0:T(8,128)(2,1)}, u32[]{:S(2)}, u32[]{:S(2)}) collective-permute-start(bf16[512,1152]{1,0:T(8,128)(2,1)} %fusion.21), channel_id=1, source_target_pairs={{0,4},{4,0},{1,5},{5,1},{2,6},{6,2},{3,7},{7,3},{8,12},{12,8},{9,1... | collective-permute-start | bytes 3538952 | tf_op jit(solution)/shard_map/ppermute | solution.py:20
  185.5 18.0 %copy-start.1 = (bf16[1024,1152]{1,0:T(8,128)(2,1)}, bf16[1024,1152]{1,0:T(8,128)(2,1)S(1)}, u32[]{:S(2)}) copy-start(bf16[1024,1152]{1,0:T(8,128)(2,1)S(1)} %dynamic_update_slice.3) | copy-start | bytes 7077892
  199.0 4.5 %copy-start.3 = (f32[1024,64]{1,0:T(8,128)S(1)}, f32[1024,64]{1,0:T(8,128)}, u32[]{:S(2)}) copy-start(f32[1024,64]{1,0:T(8,128)} %get-tuple-element.16) | copy-start | bytes 786436
  199.0 4.5 %copy-start.4 = (f32[1024,64]{1,0:T(8,128)S(1)}, f32[1024,64]{1,0:T(8,128)}, u32[]{:S(2)}) copy-start(f32[1024,64]{1,0:T(8,128)} %get-tuple-element.17) | copy-start | bytes 786436
  199.0 4.5 %copy-start.5 = (f32[1024,64]{1,0:T(8,128)S(1)}, f32[1024,64]{1,0:T(8,128)}, u32[]{:S(2)}) copy-start(f32[1024,64]{1,0:T(8,128)} %get-tuple-element.14) | copy-start | bytes 786436
  199.0 4.5 %copy-start.6 = (f32[1024,64]{1,0:T(8,128)S(1)}, f32[1024,64]{1,0:T(8,128)}, u32[]{:S(2)}) copy-start(f32[1024,64]{1,0:T(8,128)} %get-tuple-element.15) | copy-start | bytes 786436
  203.5 2.0 copy-start
  230.4 10.1 %copy-start.2 = (bf16[512,896]{1,0:T(8,128)(2,1)S(1)}, bf16[512,896]{1,0:T(8,128)(2,1)}, u32[]{:S(2)}) copy-start(bf16[512,896]{1,0:T(8,128)(2,1)} %copy.58) | copy-start | bytes 2752516
Sparse Core Ops, SparseCore 0:
  10.0 83.9 all-gather.5
  95.8 46.9 all-gather.3

commit v2 on v1

--- a/solution.py
+++ b/solution.py
@@ -1,7 +1,12 @@
+import functools
+
 import jax
 import jax.numpy as jnp
 from jax import lax
 from jax.sharding import PartitionSpec as P
+from jax.experimental import pallas as pl
+from jax.experimental.pallas import tpu as pltpu
+import numpy as np
 
 HEADS = 28
 KVH = 4
@@ -66,63 +71,85 @@
     return lax.dynamic_update_slice(padded, second_part, (first_len, jnp.int32(0)))
 
 
+QUERY_BLOCK = 256
+
+
+def attend_kernel(total_ref, proj_ref, cos_ref, sin_ref, out_ref, keys_ref, *, q_heads, head_dim):
+    length = proj_ref.shape[0]
+    total = total_ref[0]
+    root = np.float32(np.sqrt(np.float32(head_dim)))
+    lane = lax.broadcasted_iota(jnp.int32, (1, head_dim), 1)
+    half = head_dim // 2
+
+    def rope(x, c, s):
+        turned = pltpu.roll(x, half, 1)
+        turned = jnp.where(lane < half, -turned, turned)
+        return (x * c + turned * s).astype(jnp.bfloat16)
+
+    key_col = q_heads * head_dim
+    keys_ref[...] = rope(
+        proj_ref[:, key_col : key_col + head_dim].astype(jnp.float32), cos_ref[...], sin_ref[...]
+    )
+    value_col = key_col + head_dim
+    for start in range(0, length, QUERY_BLOCK):
+        stop = start + QUERY_BLOCK
+        c = cos_ref[start:stop, :]
+        s = sin_ref[start:stop, :]
+        row = start + lax.broadcasted_iota(jnp.int32, (QUERY_BLOCK, stop), 0)
+        col = lax.broadcasted_iota(jnp.int32, (QUERY_BLOCK, stop), 1)
+        allowed = (col <= row) & (col < total)
+        live = (start + lax.broadcasted_iota(jnp.int32, (QUERY_BLOCK, 1), 0)) < total
+
+        def one_head(h, carry):
+            cols = pl.ds(pl.multiple_of(h * head_dim, head_dim), head_dim)
+            q = rope(proj_ref[start:stop, cols].astype(jnp.float32), c, s)
+            scores = lax.dot_general(
+                q, keys_ref[0:stop, :], (((1,), (1,)), ((), ())),
+                preferred_element_type=jnp.float32,
+            ) / root
+            scores = jnp.where(allowed, scores, -jnp.inf)
+            largest = jnp.max(scores, axis=1, keepdims=True)
+            exponent = jnp.exp(scores - largest)
+            probs = (exponent / jnp.sum(exponent, axis=1, keepdims=True)).astype(jnp.bfloat16)
+            mixture = jnp.dot(
+                probs, proj_ref[0:stop, value_col : value_col + head_dim],
+                preferred_element_type=jnp.float32,
+            )
+            out_ref[start:stop, cols] = jnp.where(live, mixture, 0.0).astype(out_ref.dtype)
+            return carry
+
+        lax.fori_loop(0, q_heads, one_head, 0)
+
+
 def attention(projected, total_len, q_heads, kv_heads, head_dim):
     length = projected.shape[0]
     cosine, sine_table = rope_tables(length, head_dim)
-    queries = rotate(
-        projected[:, : q_heads * head_dim].reshape(length, q_heads, head_dim), cosine, sine_table
-    )
-    key_heads = rotate(
-        projected[:, q_heads * head_dim : (q_heads + kv_heads) * head_dim].reshape(
-            length, kv_heads, head_dim
+    body = functools.partial(attend_kernel, q_heads=q_heads, head_dim=head_dim)
+    flops = 2 * 2 * q_heads * head_dim * length * length // 2
+    return pl.pallas_call(
+        body,
+        out_shape=jax.ShapeDtypeStruct((length, q_heads * head_dim), projected.dtype),
+        in_specs=[
+            pl.BlockSpec(memory_space=pltpu.SMEM),
+            pl.BlockSpec(memory_space=pltpu.VMEM),
+            pl.BlockSpec(memory_space=pltpu.VMEM),
+            pl.BlockSpec(memory_space=pltpu.VMEM),
+        ],
+        out_specs=pl.BlockSpec(memory_space=pltpu.VMEM),
+        scratch_shapes=[pltpu.VMEM((length, head_dim), jnp.bfloat16)],
+        cost_estimate=pl.CostEstimate(
+            flops=flops,
+            transcendentals=q_heads * length * length // 2,
+            bytes_accessed=projected.size * 2 + length * q_heads * head_dim * 2,
         ),
-        cosine,
-        sine_table,
-    )
-    value_heads = projected[:, (q_heads + kv_heads) * head_dim :].reshape(
-        length, kv_heads, head_dim
-    )
-    grouped = queries.reshape(length, kv_heads, q_heads // kv_heads, head_dim)
-    block_length = min(BLOCK_ROWS, length)
-    root_dim = jnp.sqrt(jnp.float32(head_dim))
-    pieces = []
-    for row_start in range(0, length, block_length):
-        row_stop = row_start + block_length
-        scores = (
-            jnp.einsum(
-                "qkgd,skd->kgqs",
-                grouped[row_start:row_stop],
-                key_heads[:row_stop],
-                preferred_element_type=jnp.float32,
-            )
-            / root_dim
-        )
-        row_ids = jnp.arange(row_start, row_stop, dtype=jnp.int32)[:, None]
-        col_ids = jnp.arange(row_stop, dtype=jnp.int32)[None, :]
-        allowed = (col_ids <= row_ids) & (col_ids < total_len)
-        scores = jnp.where(allowed, scores, -jnp.inf)
-        largest = jnp.max(scores, axis=-1, keepdims=True)
-        exponent = jnp.exp(scores - largest)
-        probabilities = (exponent / jnp.sum(exponent, axis=-1, keepdims=True)).astype(jnp.bfloat16)
-        mixture = jnp.einsum(
-            "kgqs,skd->qkgd",
-            probabilities,
-            value_heads[:row_stop],
-            preferred_element_type=jnp.float32,
-        )
-        live_rows = (jnp.arange(row_start, row_stop, dtype=jnp.int32) < total_len)[
-            :, None, None, None
-        ]
-        mixture = jnp.where(live_rows, mixture, 0.0)
-        pieces.append(mixture.astype(jnp.bfloat16).reshape(block_length, q_heads * head_dim))
-    return jnp.concatenate(pieces, axis=0)
+    )(total_len.reshape(1).astype(jnp.int32), projected, cosine, sine_table)
 
 
 def shards(storage, row_doc, row_pos, doc_len, partner, norm_gain, qkv_weight, qkv_bias):
-    pair_count = lax.axis_size("pair")
+    pair_count = lax.axis_size("outer") * lax.axis_size("inner")
     doc_count = 2 * pair_count
     core = lax.axis_index("core")
-    me_index = lax.axis_index("pair") * 2 + core
+    me_index = (lax.axis_index("outer") * lax.axis_size("inner") + lax.axis_index("inner")) * 2 + core
     half_rows = HALF
     per_dest = half_rows // doc_count
     scorer, own_doc = pairing(partner)
@@ -148,7 +175,7 @@
         .set(row_pos, mode="drop")
     )
     send_pos = send_pos.reshape(doc_count, per_dest)
-    doc_axes = ("pair", "core")
+    doc_axes = ("outer", "inner", "core")
     got_rows, got_pos = (
         lax.all_to_all(send_rows, doc_axes, split_axis=0, concat_axis=0, tiled=True),
         lax.all_to_all(send_pos, doc_axes, split_axis=0, concat_axis=0, tiled=True),
@@ -161,7 +188,9 @@
     bias_wide = qkv_bias.astype(jnp.float32)
     own_full = lax.all_gather(own_rows, "tp", axis=1, tiled=True)
     normed = rms_norm(own_full, norm_gain)
-    mine = lax.all_gather(qkv_weight, "pair", axis=0, tiled=False)
+    mine = lax.all_gather(qkv_weight, "inner", axis=0, tiled=False)
+    mine = lax.all_gather(mine, "outer", axis=0, tiled=False)
+    mine = mine.reshape((-1,) + qkv_weight.shape)
     theirs = from_partner(mine, "core", 0)
     is_first = core == 0
     low = jnp.where(is_first, mine, theirs)
@@ -176,10 +205,12 @@
 
 def solution(mesh):
     doc_count, tp_count = mesh.shape["doc"], mesh.shape["tp"]
+    pairs = doc_count // 2
+    inner = 4 if pairs % 4 == 0 else 1
     split = jax.sharding.Mesh(
-        mesh.devices.reshape(doc_count // 2, 2, tp_count), ("pair", "core", "tp")
-    )
-    rows = ("pair", "core")
+        mesh.devices.reshape(pairs // inner, inner, 2, tp_count), ("outer", "inner", "core", "tp")
+    )
+    rows = ("outer", "inner", "core")
     placed = (P(rows, "tp"), P(rows), P(rows), P(), P(), P(), P(rows, "tp"), P("tp"))
     return jax.shard_map(
         shards, mesh=split, in_specs=placed, out_specs=P(rows, "tp"), check_vma=False

time: 250 us -> 221 us (0.88)
  Pallas kernels: 0 us -> 23.2 us
  other arithmetic: 49.6 us -> 28.8 us
  matrix products: 30.8 us -> 10.4 us
  local copies, waits for them, and re-layouts: 36.4 us -> 20.9 us
  blocking collectives: 0 us -> 13.4 us
  waiting for transfers between devices: 91.9 us -> 87 us
  starting transfers between devices: 23.3 us -> 19.8 us
    pallas_call x0 -> x1, Pallas kernels: none -> 23.2 us  [attention(): pl.pallas_call(body, out_shape=jax.ShapeDtypeStruct((length, q_heads * he...]
    dot_general x4 -> x0, matrix products: 20.3 us -> none  [the longest x2 12.6 us: attention(): jnp.einsum('kgqs,skd->qkgd', probabilities, value_heads[:row_stop], prefe...]
    all_gather x1, waiting for transfers between devices: 18.9 us -> 1.51 us  [shards(): mine = lax.all_gather(mine, 'outer', axis=0, tiled=False)]
    all_gather x0 -> x1, blocking collectives: none -> 13.4 us  [shards(): mine = lax.all_gather(qkv_weight, 'inner', axis=0, tiled=False)]
    convert_element_type x2 -> x0, local copies, waits for them, and re-layouts: 10.1 us -> none  [rotate(): widened = heads.astype(jnp.float32)]
    reduce_sum x2 -> x0, other arithmetic: 9.7 us -> none  [attention(): jnp.sum(exponent, axis=-1, keepdims=True)]
    all_to_all x1, waiting for transfers between devices: 24.7 us -> 33.9 us  [shards(): lax.all_to_all(send_rows, doc_axes, split_axis=0, concat_axis=0, tiled=True)]
    neg x1 -> x0, other arithmetic: 4.48 us -> none  [rotate(): -widened[..., half_dim:]]
  transfers between devices with their start and end apart: 6 -> 6, of which waited for: 4 -> 4; matrix products, arithmetic and copies ran while one was open for 12% -> 14% of each run, Pallas kernels for 0% -> 0%
where the time goes in v2:
time: 221 us; the launch traced here: 220 us
  waiting for transfers between devices  87 us (39%)
  other arithmetic  28.8 us (13%)
  Pallas kernels  23.2 us (10%)
  local copies, waits for them, and re-layouts  20.9 us (9%)
  starting transfers between devices  19.8 us (9%)
  between operations  16.4 us (7%)
  blocking collectives  13.4 us (6%)
  matrix products  10.4 us (5%)
    all_gather x1, waiting for transfers between devices, shards(): own_full = lax.all_gather(own_rows, 'tp', axis=1, tiled=True)  46.2 us
    all_to_all x1, waiting for transfers between devices, shards(): lax.all_to_all(send_rows, doc_axes, split_axis=0, concat_axis=0, tiled=True)  33.9 us
    pallas_call x1, Pallas kernels, attention(): pl.pallas_call(body, out_shape=jax.ShapeDtypeStruct((length, q_heads * he...  23.2 us
    all_gather x1, blocking collectives, shards(): mine = lax.all_gather(qkv_weight, 'inner', axis=0, tiled=False)  13.4 us
    all_to_all x1, starting transfers between devices, shards(): lax.all_to_all(send_pos, doc_axes, split_axis=0, concat_axis=0, tiled=True)  13.4 us
    another operation x2, other arithmetic, shards(): jnp.stack([low, high], axis=1).reshape(-1, qkv_weight.shape[1])  11.3 us
    dot_general x1, matrix products, shards(): own_sum = jnp.dot(normed, full_weight, preferred_element_type=jnp.float32)  10.4 us
    scatter x2, local copies, waits for them, and re-layouts, place_rows(): return blank_rows.at[dest_index].set(values, mode='drop')  7.93 us
  transfers between devices with their start and end apart: 6, of which 4 were waited for; matrix products, arithmetic and copies ran while one was open for 14% of the time, Pallas kernels for 0%

profile of v2, /device:TPU:1, one launch (start us, length us, event | category | flops | bytes accessed | tf_op | source)
XLA Modules:
  0.0 219.9 jit_solution(2470450583912472273)
XLA Ops:
  6.5 13.4 %all-gather = bf16[224,1152]{1,0:T(8,128)(2,1)} all-gather(bf16[56,1152]{1,0:T(8,128)(2,1)} %param.14), channel_id=2, replica_groups=mesh['outer'=8,'inner'=4,'core'=2,'tp'=4] {'inner'}, dimensions={0}, use_global_device_ids=true | all-gather | bytes 645120 | tf_op jit(solution)/shard_map/all_gather | solution.py:191
  20.0 0.0 all-gather.7.cloned.1.call-update
  20.0 0.7 fusion.32
  20.6 0.1 copy.17
  20.7 0.1 reduce-window.19
  20.8 0.1 reduce
  20.9 0.7 iota_minimum_fusion
  21.6 0.2 select_reduce_fusion.2
  21.8 0.7 add_subtract_fusion
  22.5 0.8 select_reduce_fusion
  23.2 0.7 fusion.34
  23.9 1.2 reduce-window.20
  25.2 0.2 slice_reduce_fusion
  25.4 0.7 broadcast_compare_fusion
  26.1 0.1 fusion.21
  26.2 0.7 compare_select_fusion.1
  26.9 2.6 %scatter_custom_fusion = s32[512]{0:T(512)S(1)} fusion(s32[512]{0:T(512)S(1)} %compare_select_fusion.1, s32[512]{0:T(512)} %param.10, s32[]{:T(128)} %constant.52.clone.1), kind=kCustom, calls=%fused_computation.51 | custom fusion | bytes 2560 | tf_op jit(solution)/shard_map/scatter | solution.py:175
  29.5 0.7 all_to_all.9
  30.2 13.4 %all-to-all-start = ((s32[64,1,8]{2,1,0:T(1,128)}), s32[64,1,8]{2,1,0:T(1,128)S(1)}, u32[]{:S(2)}, u32[]{:S(2)}) async-start(s32[64,1,8]{2,1,0:T(1,128)} %bitcast.5), calls=%async_computation | async-start | bytes 65536 | tf_op jit(solution)/shard_map/all_to_all | solution.py:181
  43.6 4.3 %scatter_custom_fusion.1 = bf16[512,896]{1,0:T(8,128)(2,1)} fusion(s32[512]{0:T(512)S(1)} %compare_select_fusion.1, bf16[512,896]{1,0:T(8,128)(2,1)} %param.8, bf16[]{:T(256)} %constant.51.clone.1), kind=kCustom, calls=%fused_computation.24 | custom fusion | bytes 918016 | tf_op jit(solution)/shard_map/scatter | solution.py:66
  47.9 5.4 %all-to-all-done = s32[64,1,8]{2,1,0:T(1,128)S(1)} async-done(((s32[64,1,8]{2,1,0:T(1,128)}), s32[64,1,8]{2,1,0:T(1,128)S(1)}, u32[]{:S(2)}, u32[]{:S(2)}) %all-to-all-start) | async-done | bytes 2080 | tf_op jit(solution)/shard_map/all_to_all | solution.py:181
  53.3 4.9 %all-to-all-start.1 = ((bf16[64,8,896]{2,1,0:T(8,128)(2,1)}), bf16[64,8,896]{2,1,0:T(8,128)(2,1)S(1)}, u32[]{:S(2)}, u32[]{:S(2)}) async-start(bf16[64,8,896]{2,1,0:T(8,128)(2,1)} %bitcast.7), calls=%async_computation.1 | async-start | bytes 1835008 | tf_op jit(solution)/shard_map/all_to_all | solution.py:180
  58.2 0.0 all-gather.5.cloned.1.call-start
  58.2 0.6 broadcast.109
  58.8 0.7 reduce.6
  59.5 0.1 reshape.123
  59.6 33.9 %all-to-all-done.1 = bf16[64,8,896]{2,1,0:T(8,128)(2,1)S(1)} async-done(((bf16[64,8,896]{2,1,0:T(8,128)(2,1)}), bf16[64,8,896]{2,1,0:T(8,128)(2,1)S(1)}, u32[]{:S(2)}, u32[]{:S(2)}) %all-to-all-start.1) | async-done | bytes 917536 | tf_op jit(solution)/shard_map/all_to_all | solution.py:180
  93.5 3.6 %scatter_custom_fusion.2 = bf16[512,896]{1,0:T(8,128)(2,1)} fusion(s32[512]{0:T(512)S(1)} %bitcast.39, bf16[64,8,896]{2,1,0:T(8,128)(2,1)S(1)} %all-to-all-done.1, bf16[]{:T(256)} %constant.51.clone.1), kind=kCustom, calls=%fused_computation.16 | custom fusion | bytes 1835010 | tf_op jit(solution)/shard_map/scatter | solution.py:66
  97.2 0.0 all-gather.5.cloned.1.call-update
  97.2 1.5 all-gather.7.cloned.1.call-done
  98.7 0.7 collective-permute-start
  99.4 46.2 %all-gather.5.cloned.1.call-done = bf16[512,3584]{1,0:T(8,128)(2,1)} async-done(((bf16[512,896]{1,0:T(8,128)(2,1)}), bf16[512,3584]{1,0:T(8,128)(2,1)}) %all-gather.5.cloned.1.call-update) | async-done | bytes 3670032 | tf_op jit(solution)/shard_map/all_gather | solution.py:189
  145.6 2.8 %fusion = f32[512]{0:T(512)S(1)} fusion(bf16[512,3584]{1,0:T(8,128)(2,1)} %all-gather.5.cloned.1.call-done), kind=kLoop, calls=%fused_computation.6 | loop fusion | flops 5504512 | bytes 3672064 | tf_op jit(solution)/shard_map/reduce_sum | solution.py:60
  148.5 5.1 %select_bitcast_fusion.1 = (bf16[32,1,56,1152]{3,2,1,0:T(8,128)(2,1)S(1)}, bf16[32,1,56,1152]{3,2,1,0:T(8,128)(2,1)}) fusion(bf16[32,56,1152]{2,1,0:T(8,128)(2,1)} %all-gather.7.cloned.1.call-done, bf16[32,56,1152]{2,1,0:T(8,128)(2,1)} %collective-permute-done, pred[]{:T(512)S(6)} %eq.110), kind=kLoop, calls=%fused_computation.10 | loop fusion | flops 4128768 | bytes 16515073 | tf_op jit(solution)/shard_map/stack | solution.py:198
  153.6 6.2 %pad_maximum_fusion = bf16[32,2,56,1152]{3,2,1,0:T(8,128)(2,1)} fusion(bf16[32,1,56,1152]{3,2,1,0:T(8,128)(2,1)} %get-tuple-element.8, bf16[32,1,56,1152]{3,2,1,0:T(8,128)(2,1)S(1)} %get-tuple-element.7), kind=kLoop, calls=%fused_computation.5 | loop fusion | flops 4128768 | bytes 16515072 | tf_op jit(solution)/shard_map/stack | solution.py:198
  159.7 10.4 %fusion.10 = bf16[512,1152]{1,0:T(8,128)(2,1)} fusion(bf16[3584,1152]{1,0:T(8,128)(2,1)} %bitcast.36, bf16[512,3584]{1,0:T(8,128)(2,1)} %all-gather.5.cloned.1.call-done, f32[3584]{0:T(1024)S(1)} %convert_element_type.28, f32[512]{0:T(512)S(1)} %add_rsqrt_fusion, f32[1152]{0:T(1024)S(1)} %convert_element_type.30), kind=kOutput, calls=%fused_computation.15 | convolution fusion | flops 4236378112 | bytes 13128192 | tf_op jit(solution)/shard_map/dot_general | solution.py:199
  170.2 0.7 collective-permute-start.1
  170.9 0.1 select_reduce_fusion.1
  171.0 0.7 fusion.29
  171.7 1.3 fusion.28
  173.0 2.0 fusion.30
  177.9 1.9 fusion.15
  179.9 1.3 pad_maximum_fusion.1
  181.2 1.4 concatenate.9
  182.6 0.0 collective-permute-done.1
  182.6 5.9 %dynamic_update_slice.3.proj_ref = bf16[1024,1152]{1,0:T(8,128)(2,1)S(1)} dynamic-update-slice(bf16[1024,1152]{1,0:T(8,128)(2,1)S(1)} %concatenate.9, bf16[512,1152]{1,0:T(8,128)(2,1)S(1)} %collective-permute-done.1, s32[]{:T(128)S(6)} %select_n.61, s32[]{:T(128)} %constant.18.clone.1) | dynamic-update-slice | bytes 2359300 | tf_op jit(solution)/shard_map/dynamic_update_slice | solution.py:71
  188.5 1.4 copy-done
  189.9 23.2 %shard_map.82 = bf16[1024,896]{1,0:T(8,128)(2,1)} custom-call(s32[1]{0:T(128)} %bitcast.1.total_ref, bf16[1024,1152]{1,0:T(8,128)(2,1)} %copy-done, f32[1024,128]{1,0:T(8,128)} %get-tuple-element.13.cos_ref, f32[1024,128]{1,0:T(8,128)} %get-tuple-element.14.sin_ref), custom_call_target="tpu_custom_call" | custom-call | flops 1879048192 | bytes 4194304 | tf_op jit(solution)/shard_map/pallas_call | solution.py:129
  (19 shorter events, 0.1 us)
Async XLA Ops:
  6.5 92.9 %copy-start.1 = (bf16[3584]{0:T(1024)(128)(2,1)S(1)}, bf16[3584]{0:T(1024)(128)(2,1)}, u32[]{:S(2)}) copy-start(bf16[3584]{0:T(1024)(128)(2,1)} %param.13) | copy-start | bytes 21508
  6.5 92.9 %copy-start.2 = (bf16[1152]{0:T(1024)(128)(2,1)S(1)}, bf16[1152]{0:T(1024)(128)(2,1)}, u32[]{:S(2)}) copy-start(bf16[1152]{0:T(1024)(128)(2,1)} %param.15) | copy-start | bytes 6916
  6.5 92.2 %all-gather.7.cloned.1.call-start = ((), (), s32[]{:S(2)}) async-start(), calls=%async_computation.3 | async-start | bytes 4644864 | tf_op jit(solution)/shard_map/all_gather | solution.py:192
  30.2 23.1 %all-to-all-start = ((s32[64,1,8]{2,1,0:T(1,128)}), s32[64,1,8]{2,1,0:T(1,128)S(1)}, u32[]{:S(2)}, u32[]{:S(2)}) async-start(s32[64,1,8]{2,1,0:T(1,128)} %bitcast.5), calls=%async_computation | async-start | bytes 65536 | tf_op jit(solution)/shard_map/all_to_all | solution.py:181
  53.3 40.2 %all-to-all-start.1 = ((bf16[64,8,896]{2,1,0:T(8,128)(2,1)}), bf16[64,8,896]{2,1,0:T(8,128)(2,1)S(1)}, u32[]{:S(2)}, u32[]{:S(2)}) async-start(bf16[64,8,896]{2,1,0:T(8,128)(2,1)} %bitcast.7), calls=%async_computation.1 | async-start | bytes 1835008 | tf_op jit(solution)/shard_map/all_to_all | solution.py:180
  58.2 87.4 %all-gather.5.cloned.1.call-start = ((), (), s32[]{:S(2)}) async-start(), calls=%async_computation.2 | async-start | bytes 4587520 | tf_op jit(solution)/shard_map/all_gather | solution.py:189
  98.7 49.8 %collective-permute-start = (bf16[32,56,1152]{2,1,0:T(8,128)(2,1)}, bf16[32,56,1152]{2,1,0:T(8,128)(2,1)}, u32[]{:S(2)}, u32[]{:S(2)}) collective-permute-start(bf16[32,56,1152]{2,1,0:T(8,128)(2,1)} %all-gather.7.cloned.1.call-done), channel_id=1, source_target_pairs={{0,4},{4,0},{1,5},{5,1},{2,6},{6,2},{3,7},{7,3},{8,12},{12,8},{9,1... | collective-permute-start | bytes 12386312 | tf_op jit(solution)/shard_map/ppermute | solution.py:25
  159.7 11.9 %copy-start.4 = (s32[64]{0:T(128)S(1)}, s32[64]{0:T(128)}, u32[]{:S(2)}) copy-start(s32[64]{0:T(128)} %param.12) | copy-start | bytes 772
  159.7 13.3 %copy-start.3 = (s32[64]{0:T(128)S(1)}, s32[64]{0:T(128)}, u32[]{:S(2)}) copy-start(s32[64]{0:T(128)} %param.11) | copy-start | bytes 772
  170.2 12.5 %collective-permute-start.1 = (bf16[512,1152]{1,0:T(8,128)(2,1)}, bf16[512,1152]{1,0:T(8,128)(2,1)S(1)}, u32[]{:S(2)}, u32[]{:S(2)}) collective-permute-start(bf16[512,1152]{1,0:T(8,128)(2,1)} %fusion.10), channel_id=1, source_target_pairs={{0,4},{4,0},{1,5},{5,1},{2,6},{6,2},{3,7},{7,3},{8,12},{12,8},{9,1... | collective-permute-start | bytes 3538952 | tf_op jit(solution)/shard_map/ppermute | solution.py:25
  188.5 1.4 copy-start
Sparse Core Ops, SparseCore 0:
  20.1 78.5 all-gather.6
  100.5 45.0 all-gather.4
